TPU v7x, 128 devices: a whole 4x4x4 slice. The times are simulated.
128 devices in a mesh: wide: 32 (over x, y, z_hi), narrow: 4 (over z_lo, core).
Axes of the slice: x: 4, y: 4, z: 4 (z_hi: 2, z_lo: 2; z = z_hi * 2 + z_lo), core: 2. Of those that a mesh axis runs over, the one named last changes fastest.
Arguments:
- coefficients: float32 [8, 8192, 8192], P(None, 'wide', 'narrow'), may hold values from -0.07 to 0.07
- tensor_blocks: float32 [8, 32, 8192], P(None, 'wide', 'narrow'), may hold values from -6 to 6
- basis_rows: float32 [32, 8192], P(None, ('wide', 'narrow')), may hold values from -1.1 to 1.1, as said below
Outputs:
- new_basis: float32 [32, 8192], P(None, ('wide', 'narrow'))
- projection: float32 [32, 32], replicated
- factor: float32 [32, 32], replicated
Inputs may be any that keep to these rules, and one draw needn't show every extreme that they name: The rows of basis_rows are nearly but not exactly orthonormal: basis_rows basis_rows^T differs from the identity by less than 0.2 in spectral norm.
All inputs are finite; a program needn't handle non-finite values.
Results may differ from a plain program's by a relative error of at most 0.0002.
Values sent between devices are 32-bit elements; how exact they have to be, the bound alone decides.
No kernel may reach another device: no remote copies, remote signals or barrier semaphores. Data moves between devices by JAX's collectives and lax.ppermute only.
A program may use at most 64 MiB of HBM per device.

v0:
```python
import jax
import jax.numpy as jnp
from jax import lax
from jax.sharding import PartitionSpec as P

N = 8192


def in_blocks(value, dim, devices):
    dims = value.shape
    parts = value.reshape(*dims[:dim], devices, dims[dim] // devices, *dims[dim + 1 :])
    return jnp.moveaxis(parts, dim, 0)


def sum_at_owner(value, axis, dim):
    devices = lax.axis_size(axis)
    parts = lax.all_to_all(in_blocks(value, dim, devices), axis, 0, 0, tiled=True)
    return jnp.sum(parts, axis=0)


def total_of_pieces(value, axis):
    parts = lax.all_gather(value, axis)
    return parts.sum(axis=0)


def body(coefficients, tensor_blocks, basis_rows):
    hi = lax.Precision.HIGHEST
    gathered = lax.all_gather(tensor_blocks, "wide", axis=1, tiled=True)
    image = sum_at_owner(
        jnp.einsum("kic,krc->ri", gathered, coefficients, precision=hi), "narrow", 0
    ).T
    local_first = jnp.dot(basis_rows, image.T, precision=hi)
    first = total_of_pieces(local_first, ("wide", "narrow"))
    once = image - jnp.dot(first.T, basis_rows, precision=hi)
    second = total_of_pieces(jnp.dot(basis_rows, once.T, precision=hi), ("wide", "narrow"))
    twice = once - jnp.dot(second.T, basis_rows, precision=hi)
    gram = total_of_pieces(jnp.dot(twice, twice.T, precision=hi), ("wide", "narrow")) / N
    factor = jnp.linalg.cholesky(gram)
    new_basis = lax.linalg.triangular_solve(factor, twice, left_side=True, lower=True)
    return (new_basis, first + second, factor)


def solution(mesh):
    in_specs = (P(None, "wide", "narrow"), P(None, "wide", "narrow"), P(None, ("wide", "narrow")))
    out_specs = (P(None, ("wide", "narrow")), P(), P())
    return jax.shard_map(body, mesh=mesh, in_specs=in_specs, out_specs=out_specs, check_vma=False)
```

profile of v0, /device:TPU:1, one launch (start us, length us, event | category | flops | bytes accessed | tf_op | source)
XLA Modules:
  0.0 235.8 jit_solution(12183286619266672822)
XLA Ops:
  7.2 1.5 copy.8
  8.7 76.6 %all-gather.5.cloned.1.call-done = f32[8,32,2048]{2,0,1:T(8,128)} async-done(((f32[8,1,2048]{2,0,1:T(8,128)}), f32[8,32,2048]{2,0,1:T(8,128)}) %all-gather.5.cloned.1.call-update) | async-done | bytes 2097168 | tf_op jit(solution)/shard_map/all_gather | solution.py:28
  85.3 18.0 %fusion.2 = f32[256,32]{0,1:T(8,128)S(1)} fusion(f32[8,256,2048]{2,1,0:T(8,128)} %param.3, f32[8,32,2048]{2,0,1:T(8,128)} %all-gather.5.cloned.1.call-done), kind=kOutput, calls=%fused_computation.2 | convolution fusion | flops 1610612736 | bytes 18907136 | tf_op jit(solution)/shard_map/kic,krc->ri/dot_general | solution.py:30
  103.5 7.4 %all_to_all.5 = f32[4,1,2048]{2,1,0:T(1,128)S(1)} all-to-all(f32[4,1,2048]{2,1,0:T(1,128)S(1)} %reshape.23), channel_id=1, replica_groups=mesh['wide'=32,'narrow'=4] {'narrow'}, dimensions={0} | all-to-all | bytes 65536 | tf_op jit(solution)/shard_map/all_to_all | solution.py:17
  110.9 0.5 broadcast.50
  111.4 0.7 reduce.6
  112.2 0.1 reshape.24
  112.3 0.1 convolution_bitcast_fusion.1
  112.5 35.7 %all-gather = f32[4096,32]{1,0:T(8,128)S(1)} all-gather(f32[32,32]{1,0:T(8,128)S(1)} %copy.11), channel_id=2, replica_groups=mesh['wide'=32,'narrow'=4] {'wide','narrow'}, dimensions={0}, use_global_device_ids=true | all-gather | bytes 528384 | tf_op jit(solution)/shard_map/all_gather | solution.py:22
  148.2 0.2 reduce_sum.39
  148.4 0.2 convolution_subtract_fusion.1
  148.6 0.1 convolution_bitcast_fusion
  148.8 35.2 %all-gather.1 = f32[4096,32]{1,0:T(8,128)S(1)} all-gather(f32[32,32]{1,0:T(8,128)S(1)} %copy.13), channel_id=3, replica_groups=mesh['wide'=32,'narrow'=4] {'wide','narrow'}, dimensions={0}, use_global_device_ids=true | all-gather | bytes 528384 | tf_op jit(solution)/shard_map/all_gather | solution.py:22
  184.0 0.2 reduce_sum.40
  184.2 0.2 convolution_subtract_fusion
  184.6 0.1 fusion.8
  184.8 35.1 %all-gather.2 = f32[4096,32]{1,0:T(8,128)S(1)} all-gather(f32[32,32]{1,0:T(8,128)S(1)} %fusion.8), channel_id=4, replica_groups=mesh['wide'=32,'narrow'=4] {'wide','narrow'}, dimensions={0}, use_global_device_ids=true | all-gather | bytes 528384 | tf_op jit(solution)/shard_map/all_gather | solution.py:22
  219.8 0.2 reduce_sum.41
  220.1 2.9 %cholesky.16 = f32[32,32]{1,0:T(8,128)S(1)} custom-call(f32[32,32]{1,0:T(8,128)S(1)} %fusion.7), custom_call_target="Cholesky" | custom-call | tf_op jit(solution)/shard_map/jit(cholesky)/cholesky | solution.py:38
  223.1 0.6 compare_reduce_fusion
  223.7 1.3 select_bitcast_fusion
  225.0 2.4 %custom-call.6 = f32[1,32,32]{1,2,0:T(8,128)S(1)} custom-call(f32[1,32,32]{2,1,0:T(8,128)S(1)} %get-tuple-element.6), custom_call_target="InvertDiagBlocksLowerTriangular" | custom-call | tf_op jit(solution)/shard_map/triangular_solve | solution.py:39
  227.4 0.8 fusion.5
  228.3 0.7 copy.16
  (16 shorter events, 0.7 us)
Async XLA Ops:
  7.2 105.1 %copy-start = (f32[32,64]{1,0:T(8,128)S(1)}, f32[32,64]{1,0:T(8,128)}, u32[]{:S(2)}) copy-start(f32[32,64]{1,0:T(8,128)} %param.5) | copy-start | bytes 24580
  7.2 78.1 %all-gather.5.cloned.1.call-start = ((), (), s32[]{:S(2)}) async-start(), calls=%async_computation.1 | async-start | bytes 2162688 | tf_op jit(solution)/shard_map/all_gather | solution.py:28
Sparse Core Ops, SparseCore 0:
  11.0 74.2 all-gather.4
where the time goes:
time: 236 us
  blocking collectives  113 us (48%)
  waiting for transfers between devices  76.6 us (32%)
  matrix products  19.7 us (8%)
  between operations  14.1 us (6%)
  other arithmetic  8.64 us (4%)
  local copies, waits for them, and re-layouts  3.34 us (1%)
    all_gather x3, blocking collectives, total_of_pieces(): parts = lax.all_gather(value, axis)  106 us
    all_gather x1, waiting for transfers between devices, body(): gathered = lax.all_gather(tensor_blocks, 'wide', axis=1, tiled=True)  76.6 us
    dot_general x1, matrix products, body(): jnp.einsum('kic,krc->ri', gathered, coefficients, precision=hi)  18 us
    all_to_all x1, blocking collectives, sum_at_owner(): lax.all_to_all(in_blocks(value, dim, devices), axis, 0, 0, tiled=True)  7.43 us
  transfers between devices with their start and end apart: 1, of which 1 were waited for; matrix products, arithmetic and copies ran while one was open for 0% of the time, Pallas kernels for 0%

commit v1 on v0

--- a/solution.py
+++ b/solution.py
@@ -25,7 +25,9 @@
 
 def body(coefficients, tensor_blocks, basis_rows):
     hi = lax.Precision.HIGHEST
-    gathered = lax.all_gather(tensor_blocks, "wide", axis=1, tiled=True)
+    gathered = jnp.concatenate(
+        lax.all_to_all(jnp.stack([tensor_blocks] * lax.axis_size("wide")), "wide", 0, 0), axis=1
+    )
     image = sum_at_owner(
         jnp.einsum("kic,krc->ri", gathered, coefficients, precision=hi), "narrow", 0
     ).T

time: 236 us -> 188 us (0.80)
  waiting for transfers between devices: 76.6 us -> 0 us
  blocking collectives: 113 us -> 154 us
  between operations: 14.1 us -> 0.74 us
    all_gather x1 -> x0, waiting for transfers between devices: 76.6 us -> none  [body(): gathered = lax.all_gather(tensor_blocks, 'wide', axis=1, tiled=True)]
    all_to_all x0 -> x1, blocking collectives: none -> 39.9 us  [body(): lax.all_to_all(jnp.stack([tensor_blocks] * lax.axis_size('wide')), 'wide'...]
  transfers between devices with their start and end apart: 1 -> 0, of which waited for: 1 -> 0; matrix products, arithmetic and copies ran while one was open for 0% -> 0% of each run, Pallas kernels for 0% -> 0%
where the time goes in v1:
time: 188 us; the launch traced here: 187 us
  blocking collectives  154 us (82%)
  matrix products  21.4 us (11%)
  other arithmetic  8.64 us (5%)
  local copies, waits for them, and re-layouts  2.86 us (2%)
    all_gather x3, blocking collectives, total_of_pieces(): parts = lax.all_gather(value, axis)  106 us
    all_to_all x1, blocking collectives, body(): lax.all_to_all(jnp.stack([tensor_blocks] * lax.axis_size('wide')), 'wide'...  39.9 us
    dot_general x1, matrix products, body(): jnp.einsum('kic,krc->ri', gathered, coefficients, precision=hi)  19.7 us
    all_to_all x1, blocking collectives, sum_at_owner(): lax.all_to_all(in_blocks(value, dim, devices), axis, 0, 0, tiled=True)  7.78 us

profile of v1, /device:TPU:1, one launch (start us, length us, event | category | flops | bytes accessed | tf_op | source)
XLA Modules:
  0.0 187.2 jit_solution(13087958114034670367)
XLA Ops:
  0.6 0.9 copy.32
  1.5 0.2 stack.2
  1.8 39.9 %all_to_all.10 = f32[32,8,1,2048]{3,1,2,0:T(8,128)S(1)} all-to-all(f32[32,8,1,2048]{3,1,2,0:T(8,128)S(1)} %stack.2), channel_id=1, replica_groups=mesh['wide'=32,'narrow'=4] {'wide'}, dimensions={0} | all-to-all | bytes 4194304 | tf_op jit(solution)/shard_map/all_to_all | solution.py:29
  41.7 19.7 %fusion.9 = f32[4,32,64]{2,1,0:T(8,128)S(1)} fusion(f32[4,64,2048,8]{2,1,0,3:T(8,128)} %bitcast.57, f32[32,8,1,2048]{3,1,2,0:T(8,128)S(1)} %all_to_all.10), kind=kOutput, calls=%fused_computation.19 | convolution fusion | flops 1610612736 | bytes 18907136 | tf_op jit(solution)/shard_map/kic,krc->ri/dot_general | solution.py:32
  61.4 7.8 %all_to_all.11 = f32[4,1,2048]{2,1,0:T(1,128)S(1)} all-to-all(f32[4,1,2048]{2,1,0:T(1,128)S(1)} %reshape.33), channel_id=1, replica_groups=mesh['wide'=32,'narrow'=4] {'narrow'}, dimensions={0} | all-to-all | bytes 65536 | tf_op jit(solution)/shard_map/all_to_all | solution.py:17
  69.2 0.5 broadcast.53
  69.7 0.7 reduce.6
  70.6 0.1 convolution_bitcast_fusion.1
  70.8 35.6 %all-gather = f32[4096,32]{1,0:T(8,128)S(1)} all-gather(f32[32,32]{1,0:T(8,128)S(1)} %copy.11), channel_id=2, replica_groups=mesh['wide'=32,'narrow'=4] {'wide','narrow'}, dimensions={0}, use_global_device_ids=true | all-gather | bytes 528384 | tf_op jit(solution)/shard_map/all_gather | solution.py:22
  106.4 0.2 reduce_sum.39
  106.6 0.2 convolution_subtract_fusion.1
  106.9 0.1 convolution_bitcast_fusion
  107.1 35.2 %all-gather.1 = f32[4096,32]{1,0:T(8,128)S(1)} all-gather(f32[32,32]{1,0:T(8,128)S(1)} %copy.13), channel_id=3, replica_groups=mesh['wide'=32,'narrow'=4] {'wide','narrow'}, dimensions={0}, use_global_device_ids=true | all-gather | bytes 528384 | tf_op jit(solution)/shard_map/all_gather | solution.py:22
  142.3 0.2 reduce_sum.40
  142.5 0.2 convolution_subtract_fusion
  142.9 0.1 fusion.12
  143.0 35.1 %all-gather.2 = f32[4096,32]{1,0:T(8,128)S(1)} all-gather(f32[32,32]{1,0:T(8,128)S(1)} %fusion.12), channel_id=4, replica_groups=mesh['wide'=32,'narrow'=4] {'wide','narrow'}, dimensions={0}, use_global_device_ids=true | all-gather | bytes 528384 | tf_op jit(solution)/shard_map/all_gather | solution.py:22
  178.1 0.2 reduce_sum.41
  178.4 2.9 %cholesky.16 = f32[32,32]{1,0:T(8,128)S(1)} custom-call(f32[32,32]{1,0:T(8,128)S(1)} %fusion.8), custom_call_target="Cholesky" | custom-call | tf_op jit(solution)/shard_map/jit(cholesky)/cholesky | solution.py:40
  181.3 0.6 compare_reduce_fusion
  182.0 1.3 select_bitcast_fusion
  183.2 2.4 %custom-call.6 = f32[1,32,32]{1,2,0:T(8,128)S(1)} custom-call(f32[1,32,32]{2,1,0:T(8,128)S(1)} %get-tuple-element.6), custom_call_target="InvertDiagBlocksLowerTriangular" | custom-call | tf_op jit(solution)/shard_map/triangular_solve | solution.py:41
  185.7 0.8 fusion.6
  186.5 0.7 copy.16
  (13 shorter events, 0.6 us)
Async XLA Ops:
  0.6 69.9 %copy-start = (f32[32,64]{1,0:T(8,128)S(1)}, f32[32,64]{1,0:T(8,128)}, u32[]{:S(2)}) copy-start(f32[32,64]{1,0:T(8,128)} %param.5) | copy-start | bytes 24580
